TPU v7x, 32 devices: a whole 2x2x4 slice. The times are simulated.
32 devices in a mesh: dp: 2 (over x), cluster: 16 (over z, y, core).
Axes of the slice: x: 2, y: 2, z: 4, core: 2. Of those that a mesh axis runs over, the one named last changes fastest.
Arguments:
- queries: bfloat16 [4096, 768], P(('dp', 'cluster')), may hold values from -6 to 6
- shortlist: int32 [4096, 8], P(('dp', 'cluster')), may hold values from 0 to 15, all different within a row; in each aligned block of 128 rows (0 to 127, 128 to 255, ...) at most 128 rows name the same one
- positives: int32 [4096, 8], P(('dp', 'cluster')), may hold values from 0 to 255
- weights: bfloat16 [16, 256, 768], P('cluster'), may hold values from -0.21875 to 0.21875
- first_moment: float32 [16, 256, 768], P('cluster'), may hold values from -24 to 24
- second_moment: float32 [16, 256, 768], P('cluster'), may hold values from 0.5 to 50
Outputs:
- new_weights: bfloat16 [16, 256, 768], P('cluster')
- new_first: float32 [16, 256, 768], P('cluster')
- new_second: float32 [16, 256, 768], P('cluster')
- query_grad: bfloat16 [4096, 768], P(('dp', 'cluster'))
Inputs may be any that keep to these rules, and one draw needn't show every extreme that they name: `shortlist`: each row names 8 different clusters. In the rows of one device no cluster is named by more than 128 rows, a bound that some block reaches of them.
All inputs are finite; a program needn't handle non-finite values.
Results may differ from a plain program's by a relative error of at most 0.0085.
Values may be sent and summed in bfloat16 or wider, within the bound.
No kernel may reach another device: no remote copies, remote signals or barrier semaphores. Data moves between devices by JAX's collectives and lax.ppermute only.
A program may use at most 64 MiB of HBM per device.

v0:
```python
import jax
import jax.numpy as jnp
from jax import lax
from jax.sharding import PartitionSpec as P

beta_one = 0.9
beta_two = 0.999
learn_rate = 0.01
adam_eps = 1e-08
adam_step = 10.0


def adam_update(cluster_weights, first_moment, second_moment, gradient):
    first_new = beta_one * first_moment + (1.0 - beta_one) * gradient
    second_new = beta_two * second_moment + (1.0 - beta_two) * gradient * gradient
    first_hat = first_new / (1.0 - beta_one**adam_step)
    second_hat = second_new / (1.0 - beta_two**adam_step)
    stepped = cluster_weights.astype(jnp.float32) - learn_rate * first_hat / (
        jnp.sqrt(second_hat) + adam_eps
    )
    return (stepped.astype(jnp.bfloat16), first_new, second_new)


def owner_work(arrived_rows, arrived_labels, cluster_rows):
    label_ids = jnp.arange(cluster_rows.shape[0], dtype=jnp.int32)
    scores = lax.dot_general(
        arrived_rows, cluster_rows, (((1,), (1,)), ((), ())), preferred_element_type=jnp.float32
    )
    target = (arrived_labels[:, None] == label_ids[None, :]).astype(jnp.float32)
    coefficient = (jax.nn.sigmoid(scores) - target).astype(jnp.bfloat16)
    gradient = lax.dot_general(
        coefficient, arrived_rows, (((0,), (0,)), ((), ())), preferred_element_type=jnp.float32
    )
    visit_grad = jnp.dot(coefficient, cluster_rows, preferred_element_type=jnp.float32).astype(
        jnp.bfloat16
    )
    return (gradient, visit_grad)


def on_device(queries, shortlist, positives, weights, first_moment, second_moment):
    owners = lax.axis_size("cluster")
    rows_dev, fanout = shortlist.shape
    feature_dim = queries.shape[1]
    capacity = min(rows_dev, 2 * rows_dev * fanout // owners)
    visits = shortlist.reshape(-1)
    labels = positives.reshape(-1)
    onehot = (visits[:, None] == jnp.arange(owners, dtype=jnp.int32)[None, :]).astype(jnp.int32)
    visit_rank = jnp.sum((jnp.cumsum(onehot, axis=0) - onehot) * onehot, axis=1)
    slot_index = visits * capacity + visit_rank
    slot_visit = (
        jnp.full((owners * capacity,), -1, jnp.int32)
        .at[slot_index]
        .set(jnp.arange(visits.shape[0], dtype=jnp.int32))
    )
    filled = slot_visit >= 0
    clamped = jnp.maximum(slot_visit, 0)
    send_rows = jnp.where(filled[:, None], queries[clamped // fanout], jnp.zeros((), queries.dtype))
    send_labels = jnp.where(filled, labels[clamped], -1)
    cluster_rows = weights[0]
    arrived_rows, arrived_labels = (
        lax.all_to_all(
            send_rows.reshape(owners, capacity, feature_dim),
            "cluster",
            split_axis=0,
            concat_axis=0,
            tiled=True,
        ),
        lax.all_to_all(
            send_labels.reshape(owners, capacity),
            "cluster",
            split_axis=0,
            concat_axis=0,
            tiled=True,
        ),
    )
    gradient, visit_grad = owner_work(
        arrived_rows.reshape(-1, feature_dim), arrived_labels.reshape(-1), cluster_rows
    )
    returned = lax.all_to_all(
        visit_grad.reshape(owners, capacity, feature_dim),
        "cluster",
        split_axis=0,
        concat_axis=0,
        tiled=True,
    )
    per_visit = returned.reshape(-1, feature_dim)[slot_index].astype(jnp.float32)
    query_grad = jnp.sum(per_visit.reshape(rows_dev, fanout, feature_dim), axis=1).astype(
        jnp.bfloat16
    )
    summed = lax.psum(gradient.astype(jnp.bfloat16), "dp").astype(jnp.float32)
    new_weights, new_first, new_second = adam_update(
        cluster_rows, first_moment[0], second_moment[0], summed
    )
    return (new_weights[None], new_first[None], new_second[None], query_grad)


def solution(mesh):
    in_specs = (
        P(("dp", "cluster"), None),
        P(("dp", "cluster"), None),
        P(("dp", "cluster"), None),
        P("cluster", None, None),
        P("cluster", None, None),
        P("cluster", None, None),
    )
    out_specs = (
        P("cluster", None, None),
        P("cluster", None, None),
        P("cluster", None, None),
        P(("dp", "cluster"), None),
    )
    return jax.shard_map(
        on_device, mesh=mesh, in_specs=in_specs, out_specs=out_specs, check_vma=False
    )
```

profile of v0, /device:TPU:13, one launch (start us, length us, event | category | flops | bytes accessed | tf_op | source)
XLA Modules:
  0.0 218.1 jit_solution(6871849412178040356)
XLA Ops:
  7.2 0.7 broadcast_multiply_fusion
  7.9 0.8 copy.13
  8.7 0.1 eq.44
  8.8 0.1 eq.40
  8.9 0.1 copy.12
  9.0 0.1 mul.63
  9.1 4.5 %reduce-window.6 = s32[16,8,128]{2,1,0:T(8,128)S(1)} reduce-window(s32[16,8,128]{2,1,0:T(8,128)S(1)} %fusion.15, s32[]{:T(128)} %constant.23.clone.1), window={size=1x1x128 pad=0_0x0_0x127_0}, to_apply=%region_0.0 | reduce-window | flops 2080768 | bytes 131076 | tf_op jit(solution)/shard_map/reduce-window
  13.6 0.1 slice.14
  13.7 0.1 copy.15
  13.9 0.1 copy.16
  13.9 0.1 broadcast_add_fusion
  14.1 4.3 %scatter_custom_fusion = s32[2048]{0:T(1024)S(1)} fusion(s32[1024]{0:T(1024)S(1)} %bitcast.72, s32[1024]{0:T(1024)S(1)} %iota.15, s32[]{:T(128)} %constant.20.clone.1), kind=kCustom, calls=%fused_computation.43 | custom fusion | bytes 8196 | tf_op jit(solution)/shard_map/scatter | solution.py:53
  18.4 0.8 copy.17
  19.2 0.1 reshape.88
  19.3 8.6 %gather_fusion.1 = s32[2048]{0:T(1024)S(1)} fusion(s32[1024]{0:T(1024)S(1)} %reshape.88, s32[2048]{0:T(1024)S(1)} %maximum_clamp_fusion), kind=kCustom, calls=%fused_computation.1 | custom fusion | bytes 24576 | tf_op jit(solution)/shard_map/gather | solution.py:58
  27.9 0.6 broadcast_select_fusion.1
  28.5 6.5 %all-to-all-start.1 = ((s32[16,1,128]{2,1,0:T(1,128)}), s32[16,1,128]{2,1,0:T(1,128)S(1)}, u32[]{:S(2)}, u32[]{:S(2)}) async-start(s32[16,1,128]{2,1,0:T(1,128)} %bitcast.9), calls=%async_computation.1 | async-start | bytes 16384 | tf_op jit(solution)/shard_map/all_to_all | solution.py:68
  35.0 9.4 %gather_fusion = bf16[2048,768]{1,0:T(8,128)(2,1)} fusion(bf16[128,768]{1,0:T(8,128)(2,1)S(1)} %copy-done, s32[2048]{0:T(1024)S(1)} %get-tuple-element.9), kind=kCustom, calls=%fused_computation | custom fusion | bytes 6299648 | tf_op jit(solution)/shard_map/gather | solution.py:57
  44.4 2.1 broadcast_select_fusion
  46.5 75.7 %all_to_all.19 = bf16[16,128,768]{2,1,0:T(8,128)(2,1)S(1)} all-to-all(bf16[16,128,768]{2,1,0:T(8,128)(2,1)S(1)} %broadcast_select_fusion), channel_id=1, replica_groups=mesh['dp'=2,'cluster'=16] {'cluster'}, dimensions={0} | all-to-all | bytes 6291456 | tf_op jit(solution)/shard_map/all_to_all | solution.py:61
  122.2 1.7 copy-done.2
  123.9 1.3 fusion.4
  125.3 2.7 %convolution_convert_fusion = bf16[2048,768]{1,0:T(8,128)(2,1)} fusion(bf16[2048,256]{1,0:T(8,128)(2,1)S(1)} %fusion.4, bf16[1,256,768]{2,1,0:T(8,128)(2,1)S(1)} %copy-done.3), kind=kOutput, calls=%fused_computation.4 | convolution fusion | flops 806879232 | bytes 4587520 | tf_op jit(solution)/shard_map/dot_general | solution.py:34
  127.9 5.1 %all-to-all-start.2 = ((bf16[16,128,768]{2,1,0:T(8,128)(2,1)}), bf16[16,128,768]{2,1,0:T(8,128)(2,1)S(1)}, u32[]{:S(2)}, u32[]{:S(2)}) async-start(bf16[16,128,768]{2,1,0:T(8,128)(2,1)} %bitcast.65), calls=%async_computation.2 | async-start | bytes 6291456 | tf_op jit(solution)/shard_map/all_to_all | solution.py:79
  133.0 0.0 all-reduce.2.cloned.1.call-start
  133.1 4.0 %convolution_convert_fusion.1 = bf16[256,768]{1,0:T(8,128)(2,1)} fusion(bf16[2048,256]{1,0:T(8,128)(2,1)} %copy-done.1, bf16[2048,768]{1,0:T(8,128)(2,1)} %bitcast.68), kind=kOutput, calls=%fused_computation.14 | convolution fusion | flops 805502976 | bytes 4587520 | tf_op jit(solution)/shard_map/dot_general | solution.py:31
  137.1 0.0 all-reduce.2.cloned.1.call-update
  137.1 26.4 %all-reduce.2.cloned.1.call-done = bf16[256,768]{1,0:T(8,128)(2,1)} async-done(((bf16[256,768]{1,0:T(8,128)(2,1)}), bf16[256,768]{1,0:T(8,128)(2,1)}) %all-reduce.2.cloned.1.call-update) | async-done | bytes 393232 | tf_op jit(solution)/shard_map/psum | solution.py:90
  163.5 3.4 %fusion.8 = (f32[1,256,768]{2,1,0:T(8,128)}, bf16[1,256,768]{2,1,0:T(8,128)(2,1)}, f32[1,256,768]{2,1,0:T(8,128)}) fusion(bf16[256,768]{1,0:T(8,128)(2,1)} %all-reduce.2.cloned.1.call-done, f32[1,256,768]{2,1,0:T(8,128)} %param.11, f32[1,256,768]{2,1,0:T(8,128)} %param.10, bf16[1,256,768]{2,1,0:T(8,128)(2,1)} %param.9), kind=kLoop, calls=%fused_computation.21 | loop fusion | flops 2949120 | bytes 4325376 | tf_op jit(solution)/shard_map/broadcast_in_dim | solution.py:94
  166.9 36.0 %all-to-all-done.2 = bf16[16,128,768]{2,1,0:T(8,128)(2,1)S(1)} async-done(((bf16[16,128,768]{2,1,0:T(8,128)(2,1)}), bf16[16,128,768]{2,1,0:T(8,128)(2,1)S(1)}, u32[]{:S(2)}, u32[]{:S(2)}) %all-to-all-start.2) | async-done | bytes 3145760 | tf_op jit(solution)/shard_map/all_to_all | solution.py:79
  202.9 5.2 %gather_fusion.2 = bf16[1024,768]{1,0:T(8,128)(2,1)} fusion(bf16[2048,768]{1,0:T(8,128)(2,1)S(1)} %bitcast.64, s32[1024]{0:T(1024)S(1)} %broadcast_clamp_fusion), kind=kCustom, calls=%fused_computation.2 | custom fusion | bytes 3149824 | tf_op jit(solution)/shard_map/gather | solution.py:86
  208.1 3.1 %bitcast_reduce_fusion = bf16[128,768]{1,0:T(8,128)(2,1)} fusion(bf16[1024,768]{1,0:T(8,128)(2,1)} %gather_fusion.2), kind=kLoop, calls=%fused_computation.13 | loop fusion | flops 688128 | bytes 1769472 | tf_op jit(solution)/shard_map/reduce_sum | solution.py:87
  (16 shorter events, 0.1 us)
Async XLA Ops:
  7.2 27.9 %copy-start = (bf16[128,768]{1,0:T(8,128)(2,1)S(1)}, bf16[128,768]{1,0:T(8,128)(2,1)}, u32[]{:S(2)}) copy-start(bf16[128,768]{1,0:T(8,128)(2,1)} %param.6) | copy-start | bytes 589828
  28.5 18.0 %all-to-all-start.1 = ((s32[16,1,128]{2,1,0:T(1,128)}), s32[16,1,128]{2,1,0:T(1,128)S(1)}, u32[]{:S(2)}, u32[]{:S(2)}) async-start(s32[16,1,128]{2,1,0:T(1,128)} %bitcast.9), calls=%async_computation.1 | async-start | bytes 16384 | tf_op jit(solution)/shard_map/all_to_all | solution.py:68
  46.5 77.4 %copy-start.3 = (bf16[1,256,768]{2,1,0:T(8,128)(2,1)S(1)}, bf16[1,256,768]{2,1,0:T(8,128)(2,1)}, u32[]{:S(2)}) copy-start(bf16[1,256,768]{2,1,0:T(8,128)(2,1)} %param.9) | copy-start | bytes 1179652
  122.2 1.7 copy-start.2
  125.3 2.7 %copy-start.1 = (bf16[2048,256]{1,0:T(8,128)(2,1)}, bf16[2048,256]{1,0:T(8,128)(2,1)S(1)}, u32[]{:S(2)}) copy-start(bf16[2048,256]{1,0:T(8,128)(2,1)S(1)} %fusion.4) | copy-start | bytes 3145732
  127.9 75.0 %all-to-all-start.2 = ((bf16[16,128,768]{2,1,0:T(8,128)(2,1)}), bf16[16,128,768]{2,1,0:T(8,128)(2,1)S(1)}, u32[]{:S(2)}, u32[]{:S(2)}) async-start(bf16[16,128,768]{2,1,0:T(8,128)(2,1)} %bitcast.65), calls=%async_computation.2 | async-start | bytes 6291456 | tf_op jit(solution)/shard_map/all_to_all | solution.py:79
  133.0 30.4 %all-reduce.2.cloned.1.call-start = ((), (), s32[]{:S(2)}) async-start(), calls=%async_computation.3 | async-start | bytes 786432 | tf_op jit(solution)/shard_map/psum | solution.py:90
Sparse Core Ops, SparseCore 0:
  137.2 26.2 all-reduce.1
where the time goes:
time: 219 us; the launch traced here: 218 us
  blocking collectives  75.7 us (35%)
  waiting for transfers between devices  62.4 us (28%)
  local copies, waits for them, and re-layouts  31.5 us (14%)
  other arithmetic  14.7 us (7%)
  between operations  14.2 us (6%)
  starting transfers between devices  11.7 us (5%)
  matrix products  7.95 us (4%)
    all_to_all x1, blocking collectives, on_device(): lax.all_to_all(send_rows.reshape(owners, capacity, feature_dim), 'cluster...  75.7 us
    all_to_all x1, waiting for transfers between devices, on_device(): lax.all_to_all(visit_grad.reshape(owners, capacity, feature_dim), 'cluste...  36 us
    psum x1, waiting for transfers between devices, on_device(): summed = lax.psum(gradient.astype(jnp.bfloat16), 'dp').astype(jnp.float32)  26.4 us
    gather x1, local copies, waits for them, and re-layouts, on_device(): queries[clamped // fanout]  9.38 us
    gather x1, local copies, waits for them, and re-layouts, on_device(): send_labels = jnp.where(filled, labels[clamped], -1)  8.58 us
    all_to_all x1, starting transfers between devices, on_device(): lax.all_to_all(send_labels.reshape(owners, capacity), 'cluster', split_ax...  6.52 us
    gather x1, local copies, waits for them, and re-layouts, on_device(): returned.reshape(-1, feature_dim)[slot_index].astype(jnp.float32)  5.21 us
    all_to_all x1, starting transfers between devices, on_device(): lax.all_to_all(visit_grad.reshape(owners, capacity, feature_dim), 'cluste...  5.1 us
  transfers between devices with their start and end apart: 3, of which 2 were waited for; matrix products, arithmetic and copies ran while one was open for 9% of the time, Pallas kernels for 0%

commit v1 on v0

--- a/solution.py
+++ b/solution.py
@@ -1,3 +1,4 @@
+import functools
 import jax
 import jax.numpy as jnp
 from jax import lax
@@ -8,6 +9,41 @@
 learn_rate = 0.01
 adam_eps = 1e-08
 adam_step = 10.0
+
+
+def _lift_ends(local_x, dim_at, w_in):
+    piece_out = local_x.shape
+    row_out = local_x.reshape(
+        *piece_out[:dim_at], w_in, piece_out[dim_at] // w_in, *piece_out[dim_at + 1 :]
+    )
+    state_now = jnp.moveaxis(row_out, dim_at, 0)
+    return state_now
+
+
+def see_the_turns(local_array, array_dim):
+    local_array = jnp.moveaxis(local_array, 0, array_dim)
+    vec_out = local_array.shape
+    everything = local_array.reshape(
+        *vec_out[:array_dim], vec_out[array_dim] * vec_out[array_dim + 1], *vec_out[array_dim + 2 :]
+    )
+    return everything
+
+
+def balance_windows_in(sample, row_axis, chunk, u):
+    y_new, carry = (jax.lax.axis_size(row_axis), jax.lax.axis_index(row_axis))
+    current_value = _lift_ends(sample, chunk, y_new)
+    blocks_here = [current_value[carry]]
+    for dev in range(1, y_new):
+        x_next = current_value[carry ^ dev]
+        blocks_here.append(
+            jax.lax.ppermute(x_next, axis_name=row_axis, perm=[(w, w ^ dev) for w in range(y_new)])
+        )
+    current_value = jnp.stack(blocks_here)[carry ^ jnp.arange(y_new)]
+    y2 = see_the_turns(current_value, u)
+    return y2
+
+
+_define_boxes = functools.partial(balance_windows_in, row_axis="cluster", chunk=0, u=0)
 
 
 def adam_update(cluster_weights, first_moment, second_moment, gradient):
@@ -58,13 +94,7 @@
     send_labels = jnp.where(filled, labels[clamped], -1)
     cluster_rows = weights[0]
     arrived_rows, arrived_labels = (
-        lax.all_to_all(
-            send_rows.reshape(owners, capacity, feature_dim),
-            "cluster",
-            split_axis=0,
-            concat_axis=0,
-            tiled=True,
-        ),
+        _define_boxes(send_rows.reshape(owners, capacity, feature_dim)),
         lax.all_to_all(
             send_labels.reshape(owners, capacity),
             "cluster",

time: 219 us -> 227 us (1.037)
  blocking collectives: 75.7 us -> 0 us
  waiting for transfers between devices: 62.4 us -> 113 us
  starting transfers between devices: 11.7 us -> 30.5 us
  local copies, waits for them, and re-layouts: 31.5 us -> 44.5 us
    all_to_all x1 -> x0, blocking collectives: 75.7 us -> none  [on_device(): lax.all_to_all(send_rows.reshape(owners, capacity, feature_dim), 'cluster...]
    ppermute x0 -> x15, waiting for transfers between devices: none -> 50.4 us  [balance_windows_in(): jax.lax.ppermute(x_next, axis_name=row_axis, perm=[(w, w ^ dev) for w in...]
    ppermute x0 -> x15, starting transfers between devices: none -> 18.4 us  [balance_windows_in(): jax.lax.ppermute(x_next, axis_name=row_axis, perm=[(w, w ^ dev) for w in...]
    unnamed x10 -> x26, local copies, waits for them, and re-layouts: 3.3 us -> 11.2 us
    gather x0 -> x1, local copies, waits for them, and re-layouts: none -> 2.64 us  [balance_windows_in(): current_value = jnp.stack(blocks_here)[carry ^ jnp.arange(y_new)]]
  transfers between devices with their start and end apart: 3 -> 18, of which waited for: 2 -> 9; matrix products, arithmetic and copies ran while one was open for 9% -> 9% of each run, Pallas kernels for 0% -> 0%
where the time goes in v1:
time: 227 us; the launch traced here: 226 us
  waiting for transfers between devices  113 us (50%)
  local copies, waits for them, and re-layouts  44.5 us (20%)
  starting transfers between devices  30.5 us (13%)
  other arithmetic  14.7 us (6%)
  between operations  14.4 us (6%)
  matrix products  9.35 us (4%)
    ppermute x15, waiting for transfers between devices, balance_windows_in(): jax.lax.ppermute(x_next, axis_name=row_axis, perm=[(w, w ^ dev) for w in...  50.4 us
    all_to_all x1, waiting for transfers between devices, on_device(): lax.all_to_all(visit_grad.reshape(owners, capacity, feature_dim), 'cluste...  36 us
    psum x1, waiting for transfers between devices, on_device(): summed = lax.psum(gradient.astype(jnp.bfloat16), 'dp').astype(jnp.float32)  26.4 us
    ppermute x15, starting transfers between devices, balance_windows_in(): jax.lax.ppermute(x_next, axis_name=row_axis, perm=[(w, w ^ dev) for w in...  18.4 us
    unnamed x26, local copies, waits for them, and re-layouts  11.2 us
    gather x1, local copies, waits for them, and re-layouts, on_device(): queries[clamped // fanout]  9.4 us
    gather x1, local copies, waits for them, and re-layouts, on_device(): send_labels = jnp.where(filled, labels[clamped], -1)  8.58 us
    all_to_all x1, starting transfers between devices, on_device(): lax.all_to_all(visit_grad.reshape(owners, capacity, feature_dim), 'cluste...  6.13 us
  transfers between devices with their start and end apart: 18, of which 9 were waited for; matrix products, arithmetic and copies ran while one was open for 9% of the time, Pallas kernels for 0%

profile of v1, /device:TPU:13, one launch (start us, length us, event | category | flops | bytes accessed | tf_op | source)
XLA Modules:
  0.0 226.3 jit_solution(8333428123035422490)
XLA Ops:
  8.9 0.8 copy.17
  10.0 4.5 %reduce-window.6 = s32[16,8,128]{2,1,0:T(8,128)S(1)} reduce-window(s32[16,8,128]{2,1,0:T(8,128)S(1)} %fusion.15, s32[]{:T(128)} %constant.34.clone.1), window={size=1x1x128 pad=0_0x0_0x127_0}, to_apply=%region_0.0 | reduce-window | flops 2080768 | bytes 131076 | tf_op jit(solution)/shard_map/reduce-window
  15.0 4.3 %scatter_custom_fusion = s32[2048]{0:T(1024)S(1)} fusion(s32[1024]{0:T(1024)S(1)} %bitcast.135, s32[1024]{0:T(1024)S(1)} %iota.19, s32[]{:T(128)} %constant.32.clone.1), kind=kCustom, calls=%fused_computation.76 | custom fusion | bytes 8196 | tf_op jit(solution)/shard_map/scatter | solution.py:89
  19.4 8.6 %gather_fusion.2 = s32[2048]{0:T(1024)S(1)} fusion(s32[1024]{0:T(1024)S(1)} %reshape.110, s32[2048]{0:T(1024)S(1)} %maximum_clamp_fusion), kind=kCustom, calls=%fused_computation.2 | custom fusion | bytes 24576 | tf_op jit(solution)/shard_map/gather | solution.py:94
  28.6 9.4 %gather_fusion = bf16[2048,768]{1,0:T(8,128)(2,1)} fusion(bf16[128,768]{1,0:T(8,128)(2,1)S(1)} %copy-done, s32[2048]{0:T(1024)S(1)} %get-tuple-element.25), kind=kCustom, calls=%fused_computation | custom fusion | bytes 6299648 | tf_op jit(solution)/shard_map/gather | solution.py:93
  38.0 2.1 broadcast_select_fusion
  40.2 1.7 dynamic-slice_bitcast_fusion
  42.7 1.5 collective-permute-start.2
  44.4 1.6 collective-permute-start.4
  46.0 6.0 %all-to-all-start = ((s32[16,1,128]{2,1,0:T(1,128)}), s32[16,1,128]{2,1,0:T(1,128)S(1)}, u32[]{:S(2)}, u32[]{:S(2)}) async-start(s32[16,1,128]{2,1,0:T(1,128)} %bitcast.41), calls=%async_computation | async-start | bytes 16384 | tf_op jit(solution)/shard_map/all_to_all | solution.py:98
  52.9 2.8 %collective-permute-start.6 = (bf16[1,128,768]{2,1,0:T(8,128)(2,1)}, bf16[1,128,768]{2,1,0:T(8,128)(2,1)S(1)}, u32[]{:S(2)}, u32[]{:S(2)}) collective-permute-start(bf16[1,128,768]{2,1,0:T(8,128)(2,1)} %get-tuple-element.14), channel_id=1, source_target_pairs={{0,7},{1,6},{2,5},{3,4},{4,3},{5,2},{6,1},{7,0},{8,15},{9,14},{10,... | collective-permute-start | bytes 589832 | tf_op jit(solution)/shard_map/ppermute | solution.py:39
  56.3 2.1 collective-permute-start.7
  60.1 2.1 collective-permute-start.9
  62.9 4.9 %collective-permute-start.10 = (bf16[1,128,768]{2,1,0:T(8,128)(2,1)}, bf16[1,128,768]{2,1,0:T(8,128)(2,1)S(1)}, u32[]{:S(2)}, u32[]{:S(2)}) collective-permute-start(bf16[1,128,768]{2,1,0:T(8,128)(2,1)} %get-tuple-element.10), channel_id=1, source_target_pairs={{0,11},{1,10},{2,9},{3,8},{4,15},{5,14},{6,13},{7,12},{8,3},{9,2},... | collective-permute-start | bytes 589832 | tf_op jit(solution)/shard_map/ppermute | solution.py:39
  69.8 1.0 collective-permute-start.12
  71.5 19.1 %collective-permute-done.8 = bf16[1,128,768]{2,1,0:T(8,128)(2,1)S(1)} collective-permute-done((bf16[1,128,768]{2,1,0:T(8,128)(2,1)}, bf16[1,128,768]{2,1,0:T(8,128)(2,1)S(1)}, u32[]{:S(2)}, u32[]{:S(2)}) %collective-permute-start.8) | collective-permute-done | bytes 196640 | tf_op jit(solution)/shard_map/ppermute | solution.py:39
  91.3 9.8 %collective-permute-done.9 = bf16[1,128,768]{2,1,0:T(8,128)(2,1)S(1)} collective-permute-done((bf16[1,128,768]{2,1,0:T(8,128)(2,1)}, bf16[1,128,768]{2,1,0:T(8,128)(2,1)S(1)}, u32[]{:S(2)}, u32[]{:S(2)}) %collective-permute-start.9) | collective-permute-done | bytes 196640 | tf_op jit(solution)/shard_map/ppermute | solution.py:39
  102.1 3.3 %collective-permute-done.10 = bf16[1,128,768]{2,1,0:T(8,128)(2,1)S(1)} collective-permute-done((bf16[1,128,768]{2,1,0:T(8,128)(2,1)}, bf16[1,128,768]{2,1,0:T(8,128)(2,1)S(1)}, u32[]{:S(2)}, u32[]{:S(2)}) %collective-permute-start.10) | collective-permute-done | bytes 196640 | tf_op jit(solution)/shard_map/ppermute | solution.py:39
  106.0 7.7 %collective-permute-done.11 = bf16[1,128,768]{2,1,0:T(8,128)(2,1)S(1)} collective-permute-done((bf16[1,128,768]{2,1,0:T(8,128)(2,1)}, bf16[1,128,768]{2,1,0:T(8,128)(2,1)S(1)}, u32[]{:S(2)}, u32[]{:S(2)}) %collective-permute-start.11) | collective-permute-done | bytes 196640 | tf_op jit(solution)/shard_map/ppermute | solution.py:39
  114.5 3.8 %collective-permute-done.12 = bf16[1,128,768]{2,1,0:T(8,128)(2,1)S(1)} collective-permute-done((bf16[1,128,768]{2,1,0:T(8,128)(2,1)}, bf16[1,128,768]{2,1,0:T(8,128)(2,1)S(1)}, u32[]{:S(2)}, u32[]{:S(2)}) %collective-permute-start.12) | collective-permute-done | bytes 196640 | tf_op jit(solution)/shard_map/ppermute | solution.py:39
  119.0 3.1 %collective-permute-done.13 = bf16[1,128,768]{2,1,0:T(8,128)(2,1)S(1)} collective-permute-done((bf16[1,128,768]{2,1,0:T(8,128)(2,1)S(1)}, bf16[1,128,768]{2,1,0:T(8,128)(2,1)S(1)}, u32[]{:S(2)}, u32[]{:S(2)}) %collective-permute-start.13) | collective-permute-done | bytes 196640 | tf_op jit(solution)/shard_map/ppermute | solution.py:39
  122.8 3.5 %collective-permute-done.14 = bf16[1,128,768]{2,1,0:T(8,128)(2,1)S(1)} collective-permute-done((bf16[1,128,768]{2,1,0:T(8,128)(2,1)S(1)}, bf16[1,128,768]{2,1,0:T(8,128)(2,1)S(1)}, u32[]{:S(2)}, u32[]{:S(2)}) %collective-permute-start.14) | collective-permute-done | bytes 196640 | tf_op jit(solution)/shard_map/ppermute | solution.py:39
  127.0 2.6 %gather_fusion.1 = bf16[16,128,768]{2,1,0:T(8,128)(2,1)S(1)} fusion(bf16[16,128,768]{2,1,0:T(8,128)(2,1)} %bitcast.129, s32[1024]{0:T(1024)S(1)} %pad_clamp_fusion), kind=kCustom, calls=%fused_computation.1 | custom fusion | bytes 6291520 | tf_op jit(solution)/shard_map/gather | solution.py:41
  129.7 2.8 %fusion.4 = bf16[2048,256]{1,0:T(8,128)(2,1)S(1)} fusion(bf16[2048,768]{1,0:T(8,128)(2,1)S(1)} %bitcast.130, s32[2048]{0:T(1024)S(1)} %bitcast.138, bf16[1,256,768]{2,1,0:T(8,128)(2,1)} %param.9), kind=kOutput, calls=%fused_computation.12 | convolution fusion | flops 808976384 | bytes 4595712 | tf_op jit(solution)/shard_map/dot_general | solution.py:62
  132.5 2.6 %convolution_convert_fusion = bf16[2048,768]{1,0:T(8,128)(2,1)} fusion(bf16[2048,256]{1,0:T(8,128)(2,1)S(1)} %fusion.4, bf16[1,256,768]{2,1,0:T(8,128)(2,1)S(1)} %copy-done.3), kind=kOutput, calls=%fused_computation.5 | convolution fusion | flops 806879232 | bytes 4587520 | tf_op jit(solution)/shard_map/dot_general | solution.py:70
  135.1 6.1 %all-to-all-start.1 = ((bf16[16,128,768]{2,1,0:T(8,128)(2,1)}), bf16[16,128,768]{2,1,0:T(8,128)(2,1)S(1)}, u32[]{:S(2)}, u32[]{:S(2)}) async-start(bf16[16,128,768]{2,1,0:T(8,128)(2,1)} %bitcast.127), calls=%async_computation.1 | async-start | bytes 6291456 | tf_op jit(solution)/shard_map/all_to_all | solution.py:109
  141.3 4.0 %convolution_convert_fusion.1 = bf16[256,768]{1,0:T(8,128)(2,1)} fusion(bf16[2048,256]{1,0:T(8,128)(2,1)} %copy-done.1, bf16[2048,768]{1,0:T(8,128)(2,1)} %bitcast.131), kind=kOutput, calls=%fused_computation.15 | convolution fusion | flops 805502976 | bytes 4587520 | tf_op jit(solution)/shard_map/dot_general | solution.py:67
  145.3 26.4 %all-reduce.2.cloned.1.call-done = bf16[256,768]{1,0:T(8,128)(2,1)} async-done(((bf16[256,768]{1,0:T(8,128)(2,1)}), bf16[256,768]{1,0:T(8,128)(2,1)}) %all-reduce.2.cloned.1.call-update) | async-done | bytes 393232 | tf_op jit(solution)/shard_map/psum | solution.py:120
  171.7 3.4 %fusion.8 = (f32[1,256,768]{2,1,0:T(8,128)}, bf16[1,256,768]{2,1,0:T(8,128)(2,1)}, f32[1,256,768]{2,1,0:T(8,128)}) fusion(bf16[256,768]{1,0:T(8,128)(2,1)} %all-reduce.2.cloned.1.call-done, f32[1,256,768]{2,1,0:T(8,128)} %param.11, f32[1,256,768]{2,1,0:T(8,128)} %param.10, bf16[1,256,768]{2,1,0:T(8,128)(2,1)} %param.9), kind=kLoop, calls=%fused_computation.22 | loop fusion | flops 2949120 | bytes 4325376 | tf_op jit(solution)/shard_map/broadcast_in_dim | solution.py:124
  175.1 36.0 %all-to-all-done.1 = bf16[16,128,768]{2,1,0:T(8,128)(2,1)S(1)} async-done(((bf16[16,128,768]{2,1,0:T(8,128)(2,1)}), bf16[16,128,768]{2,1,0:T(8,128)(2,1)S(1)}, u32[]{:S(2)}, u32[]{:S(2)}) %all-to-all-start.1) | async-done | bytes 3145760 | tf_op jit(solution)/shard_map/all_to_all | solution.py:109
  211.1 5.2 %gather_fusion.3 = bf16[1024,768]{1,0:T(8,128)(2,1)} fusion(bf16[2048,768]{1,0:T(8,128)(2,1)S(1)} %bitcast.126, s32[1024]{0:T(1024)S(1)} %broadcast_clamp_fusion), kind=kCustom, calls=%fused_computation.3 | custom fusion | bytes 3149824 | tf_op jit(solution)/shard_map/gather | solution.py:116
  216.3 3.1 %bitcast_reduce_fusion = bf16[128,768]{1,0:T(8,128)(2,1)} fusion(bf16[1024,768]{1,0:T(8,128)(2,1)} %gather_fusion.3), kind=kLoop, calls=%fused_computation.14 | loop fusion | flops 688128 | bytes 1769472 | tf_op jit(solution)/shard_map/reduce_sum | solution.py:117
  (66 shorter events, 15.9 us)
Async XLA Ops:
  7.2 21.4 %copy-start = (bf16[128,768]{1,0:T(8,128)(2,1)S(1)}, bf16[128,768]{1,0:T(8,128)(2,1)}, u32[]{:S(2)}) copy-start(bf16[128,768]{1,0:T(8,128)(2,1)} %param.6) | copy-start | bytes 589828
  41.8 48.8 %copy-start.4 = (bf16[1,128,768]{2,1,0:T(8,128)(2,1)S(1)}, bf16[1,128,768]{2,1,0:T(8,128)(2,1)}, u32[]{:S(2)}) copy-start(bf16[1,128,768]{2,1,0:T(8,128)(2,1)} %get-tuple-element.7) | copy-start | bytes 589828
  41.8 10.2 %collective-permute-start = (bf16[1,128,768]{2,1,0:T(8,128)(2,1)}, bf16[1,128,768]{2,1,0:T(8,128)(2,1)S(1)}, u32[]{:S(2)}, u32[]{:S(2)}) collective-permute-start(bf16[1,128,768]{2,1,0:T(8,128)(2,1)} %get-tuple-element.20), channel_id=1, source_target_pairs={{0,1},{1,0},{2,3},{3,2},{4,5},{5,4},{6,7},{7,6},{8,9},{9,8},{10,11... | collective-permute-start | bytes 589832 | tf_op jit(solution)/shard_map/ppermute | solution.py:39
  42.5 10.4 %collective-permute-start.1 = (bf16[1,128,768]{2,1,0:T(8,128)(2,1)}, bf16[1,128,768]{2,1,0:T(8,128)(2,1)S(1)}, u32[]{:S(2)}, u32[]{:S(2)}) collective-permute-start(bf16[1,128,768]{2,1,0:T(8,128)(2,1)} %get-tuple-element.19), channel_id=1, source_target_pairs={{0,2},{1,3},{2,0},{3,1},{4,6},{5,7},{6,4},{7,5},{8,10},{9,11},{10,... | collective-permute-start | bytes 589832 | tf_op jit(solution)/shard_map/ppermute | solution.py:39
  42.7 13.6 %collective-permute-start.2 = (bf16[1,128,768]{2,1,0:T(8,128)(2,1)}, bf16[1,128,768]{2,1,0:T(8,128)(2,1)S(1)}, u32[]{:S(2)}, u32[]{:S(2)}) collective-permute-start(bf16[1,128,768]{2,1,0:T(8,128)(2,1)} %get-tuple-element.18), channel_id=1, source_target_pairs={{0,3},{1,2},{2,1},{3,0},{4,7},{5,6},{6,5},{7,4},{8,11},{9,10},{10,... | collective-permute-start | bytes 589832 | tf_op jit(solution)/shard_map/ppermute | solution.py:39
  44.2 14.9 %collective-permute-start.3 = (bf16[1,128,768]{2,1,0:T(8,128)(2,1)}, bf16[1,128,768]{2,1,0:T(8,128)(2,1)S(1)}, u32[]{:S(2)}, u32[]{:S(2)}) collective-permute-start(bf16[1,128,768]{2,1,0:T(8,128)(2,1)} %get-tuple-element.17), channel_id=1, source_target_pairs={{0,4},{1,5},{2,6},{3,7},{4,0},{5,1},{6,2},{7,3},{8,12},{9,13},{10,... | collective-permute-start | bytes 589832 | tf_op jit(solution)/shard_map/ppermute | solution.py:39
  44.4 15.7 %collective-permute-start.4 = (bf16[1,128,768]{2,1,0:T(8,128)(2,1)}, bf16[1,128,768]{2,1,0:T(8,128)(2,1)S(1)}, u32[]{:S(2)}, u32[]{:S(2)}) collective-permute-start(bf16[1,128,768]{2,1,0:T(8,128)(2,1)} %get-tuple-element.16), channel_id=1, source_target_pairs={{0,5},{1,4},{2,7},{3,6},{4,1},{5,0},{6,3},{7,2},{8,13},{9,12},{10,... | collective-permute-start | bytes 589832 | tf_op jit(solution)/shard_map/ppermute | solution.py:39
  46.0 83.7 %all-to-all-start = ((s32[16,1,128]{2,1,0:T(1,128)}), s32[16,1,128]{2,1,0:T(1,128)S(1)}, u32[]{:S(2)}, u32[]{:S(2)}) async-start(s32[16,1,128]{2,1,0:T(1,128)} %bitcast.41), calls=%async_computation | async-start | bytes 16384 | tf_op jit(solution)/shard_map/all_to_all | solution.py:98
  52.0 10.9 %collective-permute-start.5 = (bf16[1,128,768]{2,1,0:T(8,128)(2,1)}, bf16[1,128,768]{2,1,0:T(8,128)(2,1)S(1)}, u32[]{:S(2)}, u32[]{:S(2)}) collective-permute-start(bf16[1,128,768]{2,1,0:T(8,128)(2,1)} %get-tuple-element.15), channel_id=1, source_target_pairs={{0,6},{1,7},{2,4},{3,5},{4,2},{5,3},{6,0},{7,1},{8,14},{9,15},{10,... | collective-permute-start | bytes 589832 | tf_op jit(solution)/shard_map/ppermute | solution.py:39
  52.9 15.6 %collective-permute-start.6 = (bf16[1,128,768]{2,1,0:T(8,128)(2,1)}, bf16[1,128,768]{2,1,0:T(8,128)(2,1)S(1)}, u32[]{:S(2)}, u32[]{:S(2)}) collective-permute-start(bf16[1,128,768]{2,1,0:T(8,128)(2,1)} %get-tuple-element.14), channel_id=1, source_target_pairs={{0,7},{1,6},{2,5},{3,4},{4,3},{5,2},{6,1},{7,0},{8,15},{9,14},{10,... | collective-permute-start | bytes 589832 | tf_op jit(solution)/shard_map/ppermute | solution.py:39
  56.3 13.4 %collective-permute-start.7 = (bf16[1,128,768]{2,1,0:T(8,128)(2,1)}, bf16[1,128,768]{2,1,0:T(8,128)(2,1)S(1)}, u32[]{:S(2)}, u32[]{:S(2)}) collective-permute-start(bf16[1,128,768]{2,1,0:T(8,128)(2,1)} %get-tuple-element.13), channel_id=1, source_target_pairs={{0,8},{1,9},{2,10},{3,11},{4,12},{5,13},{6,14},{7,15},{8,0},{9,1},... | collective-permute-start | bytes 589832 | tf_op jit(solution)/shard_map/ppermute | solution.py:39
  59.1 31.5 %collective-permute-start.8 = (bf16[1,128,768]{2,1,0:T(8,128)(2,1)}, bf16[1,128,768]{2,1,0:T(8,128)(2,1)S(1)}, u32[]{:S(2)}, u32[]{:S(2)}) collective-permute-start(bf16[1,128,768]{2,1,0:T(8,128)(2,1)} %get-tuple-element.12), channel_id=1, source_target_pairs={{0,9},{1,8},{2,11},{3,10},{4,13},{5,12},{6,15},{7,14},{8,1},{9,0},... | collective-permute-start | bytes 589832 | tf_op jit(solution)/shard_map/ppermute | solution.py:39
  60.1 41.0 %collective-permute-start.9 = (bf16[1,128,768]{2,1,0:T(8,128)(2,1)}, bf16[1,128,768]{2,1,0:T(8,128)(2,1)S(1)}, u32[]{:S(2)}, u32[]{:S(2)}) collective-permute-start(bf16[1,128,768]{2,1,0:T(8,128)(2,1)} %get-tuple-element.11), channel_id=1, source_target_pairs={{0,10},{1,11},{2,8},{3,9},{4,14},{5,15},{6,12},{7,13},{8,2},{9,3},... | collective-permute-start | bytes 589832 | tf_op jit(solution)/shard_map/ppermute | solution.py:39
  62.9 42.5 %collective-permute-start.10 = (bf16[1,128,768]{2,1,0:T(8,128)(2,1)}, bf16[1,128,768]{2,1,0:T(8,128)(2,1)S(1)}, u32[]{:S(2)}, u32[]{:S(2)}) collective-permute-start(bf16[1,128,768]{2,1,0:T(8,128)(2,1)} %get-tuple-element.10), channel_id=1, source_target_pairs={{0,11},{1,10},{2,9},{3,8},{4,15},{5,14},{6,13},{7,12},{8,3},{9,2},... | collective-permute-start | bytes 589832 | tf_op jit(solution)/shard_map/ppermute | solution.py:39
  68.5 45.3 %collective-permute-start.11 = (bf16[1,128,768]{2,1,0:T(8,128)(2,1)}, bf16[1,128,768]{2,1,0:T(8,128)(2,1)S(1)}, u32[]{:S(2)}, u32[]{:S(2)}) collective-permute-start(bf16[1,128,768]{2,1,0:T(8,128)(2,1)} %get-tuple-element.9), channel_id=1, source_target_pairs={{0,12},{1,13},{2,14},{3,15},{4,8},{5,9},{6,10},{7,11},{8,4},{9,5},... | collective-permute-start | bytes 589832 | tf_op jit(solution)/shard_map/ppermute | solution.py:39
  69.8 48.5 %collective-permute-start.12 = (bf16[1,128,768]{2,1,0:T(8,128)(2,1)}, bf16[1,128,768]{2,1,0:T(8,128)(2,1)S(1)}, u32[]{:S(2)}, u32[]{:S(2)}) collective-permute-start(bf16[1,128,768]{2,1,0:T(8,128)(2,1)} %get-tuple-element.8), channel_id=1, source_target_pairs={{0,13},{1,12},{2,15},{3,14},{4,9},{5,8},{6,11},{7,10},{8,5},{9,4},... | collective-permute-start | bytes 589832 | tf_op jit(solution)/shard_map/ppermute | solution.py:39
  90.6 31.5 %collective-permute-start.13 = (bf16[1,128,768]{2,1,0:T(8,128)(2,1)S(1)}, bf16[1,128,768]{2,1,0:T(8,128)(2,1)S(1)}, u32[]{:S(2)}, u32[]{:S(2)}) collective-permute-start(bf16[1,128,768]{2,1,0:T(8,128)(2,1)S(1)} %copy-done.4), channel_id=1, source_target_pairs={{0,14},{1,15},{2,12},{3,13},{4,10},{5,11},{6,8},{7,9},{8,6},{9,7},... | collective-permute-start | bytes 589832 | tf_op jit(solution)/shard_map/ppermute | solution.py:39
  101.1 25.2 %collective-permute-start.14 = (bf16[1,128,768]{2,1,0:T(8,128)(2,1)S(1)}, bf16[1,128,768]{2,1,0:T(8,128)(2,1)S(1)}, u32[]{:S(2)}, u32[]{:S(2)}) collective-permute-start(bf16[1,128,768]{2,1,0:T(8,128)(2,1)S(1)} %get-tuple-element.6), channel_id=1, source_target_pairs={{0,15},{1,14},{2,13},{3,12},{4,11},{5,10},{6,9},{7,8},{8,7},{9,6},... | collective-permute-start | bytes 589832 | tf_op jit(solution)/shard_map/ppermute | solution.py:39
  129.7 2.8 %copy-start.2 = (bf16[16,128,768]{2,1,0:T(8,128)(2,1)}, bf16[16,128,768]{2,1,0:T(8,128)(2,1)S(1)}, u32[]{:S(2)}) copy-start(bf16[16,128,768]{2,1,0:T(8,128)(2,1)S(1)} %gather_fusion.1) | copy-start | bytes 9437188
  129.7 2.8 %copy-start.3 = (bf16[1,256,768]{2,1,0:T(8,128)(2,1)S(1)}, bf16[1,256,768]{2,1,0:T(8,128)(2,1)}, u32[]{:S(2)}) copy-start(bf16[1,256,768]{2,1,0:T(8,128)(2,1)} %param.9) | copy-start | bytes 1179652
  132.5 2.6 %copy-start.1 = (bf16[2048,256]{1,0:T(8,128)(2,1)}, bf16[2048,256]{1,0:T(8,128)(2,1)S(1)}, u32[]{:S(2)}) copy-start(bf16[2048,256]{1,0:T(8,128)(2,1)S(1)} %fusion.4) | copy-start | bytes 3145732
  135.1 76.0 %all-to-all-start.1 = ((bf16[16,128,768]{2,1,0:T(8,128)(2,1)}), bf16[16,128,768]{2,1,0:T(8,128)(2,1)S(1)}, u32[]{:S(2)}, u32[]{:S(2)}) async-start(bf16[16,128,768]{2,1,0:T(8,128)(2,1)} %bitcast.127), calls=%async_computation.1 | async-start | bytes 6291456 | tf_op jit(solution)/shard_map/all_to_all | solution.py:109
  141.2 30.5 %all-reduce.2.cloned.1.call-start = ((), (), s32[]{:S(2)}) async-start(), calls=%async_computation.2 | async-start | bytes 786432 | tf_op jit(solution)/shard_map/psum | solution.py:120
Sparse Core Ops, SparseCore 0:
  145.4 26.2 all-reduce.1
